TPU v7x, 512 devices: a whole 4x4x16 slice. The times are simulated.
512 devices in a mesh: group: 32 (over x, y, core), tp: 16 (over z).
Axes of the slice: x: 4, y: 4, z: 16, core: 2. Of those that a mesh axis runs over, the one named last changes fastest.
Arguments:
- tokens: bfloat16 [24576, 8192], P('group', 'tp'), may hold values from -6 to 6
- w_query: bfloat16 [8192, 4096], P(None, 'tp'), may hold values from -0.0625 to 0.0625
- adapter_down: bfloat16 [384, 16, 8192], P('group', None, 'tp'), may hold values from -0.0625 to 0.0625
- adapter_up: bfloat16 [384, 16, 4096], P('group', None, 'tp'), may hold values from -1.5 to 1.5
- adapter_id: int32 [24576], P('group'), may hold values from 0 to 383, as said below
Outputs:
- query: bfloat16 [24576, 4096], P('group', 'tp')
Inputs may be any that keep to these rules, and one draw needn't show every extreme that they name: `adapter_id`: adapter a is owned by group a // 12. Among the 768 requests of one group (an aligned block), at most 48 use adapters of any one owner; in every draw one owner receives exactly 48 from every group.
All inputs are finite; a program needn't handle non-finite values.
Results may differ from a plain program's by a relative error of at most 0.014.
Values may be sent and summed in bfloat16 or wider, within the bound.
No kernel may reach another device: no remote copies, remote signals or barrier semaphores. Data moves between devices by JAX's collectives and lax.ppermute only.
A program may use at most 128 MiB of HBM per device.

v0:
```python
import jax
import jax.numpy as jnp
from jax import lax
from jax.sharding import PartitionSpec as P

adapter_scale_factor = 2.0


def on_device(tokens, w_query, adapter_down, adapter_up, adapter_id):
    pool_down, pool_up = (
        lax.all_gather(adapter_down, "group", axis=0, tiled=True),
        lax.all_gather(adapter_up, "group", axis=0, tiled=True),
    )
    picked_down = jnp.take(pool_down, adapter_id, axis=0)
    partial_value = jnp.einsum(
        "nd,nrd->nr", tokens, picked_down, preferred_element_type=jnp.float32
    )
    total_output = lax.psum(partial_value, "tp")
    scaled_delta = (adapter_scale_factor * total_output).astype(jnp.bfloat16)
    picked_up = jnp.take(pool_up, adapter_id, axis=0)
    delta_rows = jnp.einsum(
        "nr,nrh->nh", scaled_delta, picked_up, preferred_element_type=jnp.float32
    ).astype(jnp.bfloat16)
    base = jnp.dot(
        lax.all_gather(tokens, "tp", axis=1, tiled=True),
        w_query,
        preferred_element_type=jnp.float32,
    )
    return (base + delta_rows.astype(jnp.float32)).astype(jnp.bfloat16)


def solution(mesh):
    placed = (
        P("group", "tp"),
        P(None, "tp"),
        P("group", None, "tp"),
        P("group", None, "tp"),
        P("group"),
    )
    return jax.shard_map(
        on_device, mesh=mesh, in_specs=placed, out_specs=P("group", "tp"), check_vma=False
    )
```

profile of v0, /device:TPU:1, one launch (start us, length us, event | category | flops | bytes accessed | tf_op | source)
XLA Modules:
  0.0 317.1 jit_solution(11295828361454792933)
XLA Ops:
  6.5 0.0 all-gather.8.cloned.1.call-start
  6.5 0.7 all-gather.8.cloned.1.call-update
  7.3 0.0 all-gather.6.cloned.1.call-start
  7.3 0.7 all-gather.6.cloned.1.call-update
  8.0 0.0 all-gather.4.cloned.1.call-start
  8.1 0.7 all-gather.4.cloned.1.call-update
  8.7 0.7 compare_select_fusion
  9.4 0.7 compare_and_fusion
  10.1 66.6 %all-gather.8.cloned.1.call-done = bf16[384,16,256]{2,1,0:T(8,128)(2,1)} async-done(((bf16[12,16,256]{2,1,0:T(8,128)(2,1)}), bf16[384,16,256]{2,1,0:T(8,128)(2,1)}) %all-gather.8.cloned.1.call-update) | async-done | bytes 3145744 | tf_op jit(solution)/shard_map/all_gather | solution.py:12
  76.7 7.0 %gather_fusion.1 = bf16[768,16,256]{2,1,0:T(8,128)(2,1)} fusion(bf16[384,16,256]{2,1,0:T(8,128)(2,1)} %all-gather.8.cloned.1.call-done, s32[1024]{0:T(1024)S(1)} %pad_clamp_fusion), kind=kCustom, calls=%fused_computation.1 | custom fusion | bytes 12585984 | tf_op jit(solution)/shard_map/jit(_take)/gather | solution.py:20
  83.6 0.0 copy-start
  83.6 60.0 %all-gather.6.cloned.1.call-done = bf16[384,16,512]{2,1,0:T(8,128)(2,1)} async-done(((bf16[12,16,512]{2,1,0:T(8,128)(2,1)}), bf16[384,16,512]{2,1,0:T(8,128)(2,1)}) %all-gather.6.cloned.1.call-update) | async-done | bytes 6291472 | tf_op jit(solution)/shard_map/all_gather | solution.py:11
  143.7 22.4 %gather_fusion = bf16[768,16,512]{2,1,0:T(8,128)(2,1)} fusion(bf16[384,16,512]{2,1,0:T(8,128)(2,1)} %all-gather.6.cloned.1.call-done, s32[1024]{0:T(1024)S(1)} %pad_clamp_fusion), kind=kCustom, calls=%fused_computation | custom fusion | bytes 25168896 | tf_op jit(solution)/shard_map/jit(_take)/gather | solution.py:14
  166.1 0.0 copy-done
  166.1 9.9 %fusion = f32[768,1,16]{2,1,0:T(1,128)S(1)} fusion(bf16[768,16,512]{2,1,0:T(8,128)(2,1)} %gather_fusion, pred[768]{0:T(1024)(128)(4,1)S(1)} %compare_and_fusion, bf16[768,512,1]{1,0,2:T(8,128)(2,1)S(1)} %bitcast.11), kind=kOutput, calls=%fused_computation.2 | convolution fusion | flops 18874368 | bytes 13419264 | tf_op jit(solution)/shard_map/nd,nrd->nr/dot_general | solution.py:15
  176.1 61.4 %psum.7 = f32[768,16]{1,0:T(8,128)S(1)} all-reduce(f32[768,16]{1,0:T(8,128)S(1)} %bitcast.12), channel_id=1, replica_groups=mesh['group'=32,'tp'=16] {'tp'}, use_global_device_ids=true, to_apply=%region_0.1 | all-reduce | flops 12288 | bytes 98304 | tf_op jit(solution)/shard_map/psum | solution.py:18
  237.5 8.5 %fusion.3 = bf16[768,1,256]{2,1,0:T(2,128)(2,1)S(1)} fusion(bf16[768,16,256]{2,1,0:T(8,128)(2,1)} %gather_fusion.1, pred[768]{0:T(1024)(128)(4,1)S(1)} %compare_and_fusion, bf16[768,16,1]{1,0,2:T(8,128)(2,1)S(1)} %fusion.11), kind=kOutput, calls=%fused_computation.5 | convolution fusion | flops 9437184 | bytes 6710016 | tf_op jit(solution)/shard_map/nr,nrh->nh/dot_general | solution.py:21
  246.0 54.7 %all-gather.4.cloned.1.call-done = bf16[768,8192]{1,0:T(8,128)(2,1)} async-done(((bf16[768,512]{1,0:T(8,128)(2,1)}), bf16[768,8192]{1,0:T(8,128)(2,1)}) %all-gather.4.cloned.1.call-update) | async-done | bytes 12582928 | tf_op jit(solution)/shard_map/all_gather | solution.py:25
  300.7 9.9 %fusion.9 = bf16[768,256]{1,0:T(8,128)(2,1)} fusion(bf16[768,8192]{1,0:T(8,128)(2,1)} %all-gather.4.cloned.1.call-done, bf16[8192,256]{1,0:T(8,128)(2,1)} %param.6, bf16[768,1,256]{2,1,0:T(2,128)(2,1)S(1)} %fusion.3), kind=kOutput, calls=%fused_computation.12 | convolution fusion | flops 3221815296 | bytes 17563648 | tf_op jit(solution)/shard_map/dot_general | solution.py:24
  (2 shorter events, 0.0 us)
Async XLA Ops:
  6.5 70.2 %all-gather.8.cloned.1.call-start = ((), (), s32[]{:S(2)}) async-start(), calls=%async_computation.2 | async-start | bytes 3244032 | tf_op jit(solution)/shard_map/all_gather | solution.py:12
  7.3 136.4 %all-gather.6.cloned.1.call-start = ((), (), s32[]{:S(2)}) async-start(), calls=%async_computation.1 | async-start | bytes 6488064 | tf_op jit(solution)/shard_map/all_gather | solution.py:11
  8.0 292.7 %all-gather.4.cloned.1.call-start = ((), (), s32[]{:S(2)}) async-start(), calls=%async_computation | async-start | bytes 13369344 | tf_op jit(solution)/shard_map/all_gather | solution.py:25
  83.6 82.5 %copy-start = (bf16[768,512]{1,0:T(8,128)(2,1)S(1)}, bf16[768,512]{1,0:T(8,128)(2,1)}, u32[]{:S(2)}) copy-start(bf16[768,512]{1,0:T(8,128)(2,1)} %param.5) | copy-start | bytes 2359300
Sparse Core Ops, SparseCore 0:
  10.5 66.1 all-gather.7
  79.8 63.8 all-gather.5
  145.8 154.8 all-gather.3
where the time goes:
time: 317 us
  waiting for transfers between devices  183 us (58%)
  blocking collectives  61.4 us (19%)
  local copies, waits for them, and re-layouts  29.4 us (9%)
  matrix products  28.3 us (9%)
  between operations  13.2 us (4%)
    all_gather x1, waiting for transfers between devices, on_device(): lax.all_gather(adapter_up, 'group', axis=0, tiled=True)  66.6 us
    psum x1, blocking collectives, on_device(): total_output = lax.psum(partial_value, 'tp')  61.4 us
    all_gather x1, waiting for transfers between devices, on_device(): lax.all_gather(adapter_down, 'group', axis=0, tiled=True)  60 us
    all_gather x1, waiting for transfers between devices, on_device(): lax.all_gather(tokens, 'tp', axis=1, tiled=True)  54.7 us
    gather x1, local copies, waits for them, and re-layouts, on_device(): picked_down = jnp.take(pool_down, adapter_id, axis=0)  22.4 us
    dot_general x1, matrix products, on_device(): jnp.dot(lax.all_gather(tokens, 'tp', axis=1, tiled=True), w_query, prefer...  9.92 us
    dot_general x1, matrix products, on_device(): jnp.einsum('nd,nrd->nr', tokens, picked_down, preferred_element_type=jnp....  9.91 us
    dot_general x1, matrix products, on_device(): jnp.einsum('nr,nrh->nh', scaled_delta, picked_up, preferred_element_type=...  8.51 us
  transfers between devices with their start and end apart: 3, of which 3 were waited for; matrix products, arithmetic and copies ran while one was open for 16% of the time, Pallas kernels for 0%

commit v1 on v0

--- a/solution.py
+++ b/solution.py
@@ -8,7 +8,10 @@
 
 def on_device(tokens, w_query, adapter_down, adapter_up, adapter_id):
     pool_down, pool_up = (
-        lax.all_gather(adapter_down, "group", axis=0, tiled=True),
+        jnp.concatenate(
+            lax.all_to_all(jnp.stack([adapter_down] * lax.axis_size("group")), "group", 0, 0),
+            axis=0,
+        ),
         lax.all_gather(adapter_up, "group", axis=0, tiled=True),
     )
     picked_down = jnp.take(pool_down, adapter_id, axis=0)

time: 317 us -> 289 us (0.912)
  waiting for transfers between devices: 183 us -> 137 us
  starting transfers between devices: 0.08 us -> 11.6 us
  local copies, waits for them, and re-layouts: 29.4 us -> 33.9 us
    all_to_all x0 -> x1, waiting for transfers between devices: none -> 80.9 us  [on_device(): lax.all_to_all(jnp.stack([adapter_down] * lax.axis_size('group')), 'group...]
    all_gather x1, waiting for transfers between devices: 66.6 us -> 0.02 us  [on_device(): lax.all_gather(adapter_up, 'group', axis=0, tiled=True)]
    all_gather x1 -> x0, waiting for transfers between devices: 60 us -> none  [on_device(): lax.all_gather(adapter_down, 'group', axis=0, tiled=True)]
    all_to_all x0 -> x1, starting transfers between devices: none -> 11.5 us  [on_device(): lax.all_to_all(jnp.stack([adapter_down] * lax.axis_size('group')), 'group...]
    another operation x0 -> x1, local copies, waits for them, and re-layouts: none -> 4.33 us  [on_device(): jnp.stack([adapter_down] * lax.axis_size('group'))]
  transfers between devices with their start and end apart: 3 -> 3, of which waited for: 3 -> 2; matrix products, arithmetic and copies ran while one was open for 16% -> 18% of each run, Pallas kernels for 0% -> 0%
where the time goes in v1:
time: 289 us
  waiting for transfers between devices  137 us (47%)
  blocking collectives  64.5 us (22%)
  local copies, waits for them, and re-layouts  33.9 us (12%)
  matrix products  28.3 us (10%)
  between operations  13.5 us (5%)
  starting transfers between devices  11.6 us (4%)
    all_to_all x1, waiting for transfers between devices, on_device(): lax.all_to_all(jnp.stack([adapter_down] * lax.axis_size('group')), 'group...  80.9 us
    psum x1, blocking collectives, on_device(): total_output = lax.psum(partial_value, 'tp')  64.5 us
    all_gather x1, waiting for transfers between devices, on_device(): lax.all_gather(tokens, 'tp', axis=1, tiled=True)  54.8 us
    gather x1, local copies, waits for them, and re-layouts, on_device(): picked_down = jnp.take(pool_down, adapter_id, axis=0)  22.5 us
    all_to_all x1, starting transfers between devices, on_device(): lax.all_to_all(jnp.stack([adapter_down] * lax.axis_size('group')), 'group...  11.5 us
    dot_general x1, matrix products, on_device(): jnp.dot(lax.all_gather(tokens, 'tp', axis=1, tiled=True), w_query, prefer...  9.92 us
    dot_general x1, matrix products, on_device(): jnp.einsum('nd,nrd->nr', tokens, picked_down, preferred_element_type=jnp....  9.88 us
    dot_general x1, matrix products, on_device(): jnp.einsum('nr,nrh->nh', scaled_delta, picked_up, preferred_element_type=...  8.51 us
  transfers between devices with their start and end apart: 3, of which 2 were waited for; matrix products, arithmetic and copies ran while one was open for 18% of the time, Pallas kernels for 0%

profile of v1, /device:TPU:1, one launch (start us, length us, event | category | flops | bytes accessed | tf_op | source)
XLA Modules:
  0.0 288.9 jit_solution(17714049606796339259)
XLA Ops:
  6.5 0.0 all-gather.5.cloned.1.call-start
  6.5 0.7 all-gather.5.cloned.1.call-update
  7.3 0.0 all-gather.3.cloned.1.call-start
  7.3 0.7 all-gather.3.cloned.1.call-update
  8.0 4.3 %stack.2 = bf16[32,12,16,512]{3,2,1,0:T(8,128)(2,1)} broadcast(bf16[12,16,512]{2,1,0:T(8,128)(2,1)} %param.7), dimensions={1,2,3} | broadcast | bytes 6488064 | tf_op jit(solution)/shard_map/stack | solution.py:12
  12.3 0.0 copy-start.1
  12.3 11.5 %all-to-all-start = ((bf16[32,12,16,512]{3,2,1,0:T(8,128)(2,1)}), bf16[32,12,16,512]{3,2,1,0:T(8,128)(2,1)}, u32[]{:S(2)}, u32[]{:S(2)}) async-start(bf16[32,12,16,512]{3,2,1,0:T(8,128)(2,1)} %stack.2), calls=%async_computation | async-start | bytes 12582912 | tf_op jit(solution)/shard_map/all_to_all | solution.py:12
  23.9 0.0 copy-done.1
  23.9 80.9 %all-to-all-done = bf16[32,12,16,512]{3,2,1,0:T(8,128)(2,1)} async-done(((bf16[32,12,16,512]{3,2,1,0:T(8,128)(2,1)}), bf16[32,12,16,512]{3,2,1,0:T(8,128)(2,1)}, u32[]{:S(2)}, u32[]{:S(2)}) %all-to-all-start) | async-done | bytes 6291488 | tf_op jit(solution)/shard_map/all_to_all | solution.py:12
  104.8 22.5 %gather_fusion = bf16[768,16,512]{2,1,0:T(8,128)(2,1)} fusion(bf16[384,16,512]{2,1,0:T(8,128)(2,1)} %bitcast, s32[1024]{0:T(1024)S(1)} %pad_clamp_fusion), kind=kCustom, calls=%fused_computation | custom fusion | bytes 25168896 | tf_op jit(solution)/shard_map/jit(_take)/gather | solution.py:17
  127.4 0.0 copy-start
  127.4 0.0 all-gather.5.cloned.1.call-done
  127.4 7.0 %gather_fusion.1 = bf16[768,16,256]{2,1,0:T(8,128)(2,1)} fusion(bf16[384,16,256]{2,1,0:T(8,128)(2,1)} %all-gather.5.cloned.1.call-done, s32[1024]{0:T(1024)S(1)} %pad_clamp_fusion), kind=kCustom, calls=%fused_computation.1 | custom fusion | bytes 12585984 | tf_op jit(solution)/shard_map/jit(_take)/gather | solution.py:23
  134.4 0.0 copy-done
  134.4 9.9 %fusion = f32[768,1,16]{2,1,0:T(1,128)S(1)} fusion(bf16[768,16,512]{2,1,0:T(8,128)(2,1)} %gather_fusion, pred[768]{0:T(1024)(128)(4,1)S(1)} %compare_and_fusion, bf16[768,512,1]{1,0,2:T(8,128)(2,1)S(1)} %bitcast.12), kind=kOutput, calls=%fused_computation.2 | convolution fusion | flops 18874368 | bytes 13419264 | tf_op jit(solution)/shard_map/nd,nrd->nr/dot_general | solution.py:18
  144.3 64.5 %psum.7 = f32[768,16]{1,0:T(8,128)S(1)} all-reduce(f32[768,16]{1,0:T(8,128)S(1)} %bitcast.13), channel_id=1, replica_groups=mesh['group'=32,'tp'=16] {'tp'}, use_global_device_ids=true, to_apply=%region_0.1 | all-reduce | flops 12288 | bytes 98304 | tf_op jit(solution)/shard_map/psum | solution.py:21
  208.8 8.5 %fusion.3 = bf16[768,1,256]{2,1,0:T(2,128)(2,1)S(1)} fusion(bf16[768,16,256]{2,1,0:T(8,128)(2,1)} %gather_fusion.1, pred[768]{0:T(1024)(128)(4,1)S(1)} %compare_and_fusion, bf16[768,16,1]{1,0,2:T(8,128)(2,1)S(1)} %fusion.11), kind=kOutput, calls=%fused_computation.5 | convolution fusion | flops 9437184 | bytes 6710016 | tf_op jit(solution)/shard_map/nr,nrh->nh/dot_general | solution.py:24
  217.3 54.8 %all-gather.3.cloned.1.call-done = bf16[768,8192]{1,0:T(8,128)(2,1)} async-done(((bf16[768,512]{1,0:T(8,128)(2,1)}), bf16[768,8192]{1,0:T(8,128)(2,1)}) %all-gather.3.cloned.1.call-update) | async-done | bytes 12582928 | tf_op jit(solution)/shard_map/all_gather | solution.py:28
  272.2 9.9 %fusion.9 = bf16[768,256]{1,0:T(8,128)(2,1)} fusion(bf16[768,8192]{1,0:T(8,128)(2,1)} %all-gather.3.cloned.1.call-done, bf16[8192,256]{1,0:T(8,128)(2,1)} %param.6, bf16[768,1,256]{2,1,0:T(2,128)(2,1)S(1)} %fusion.3), kind=kOutput, calls=%fused_computation.12 | convolution fusion | flops 3221815296 | bytes 17563648 | tf_op jit(solution)/shard_map/dot_general | solution.py:27
  (4 shorter events, 0.0 us)
Async XLA Ops:
  6.5 120.9 %all-gather.5.cloned.1.call-start = ((), (), s32[]{:S(2)}) async-start(), calls=%async_computation.2 | async-start | bytes 3244032 | tf_op jit(solution)/shard_map/all_gather | solution.py:15
  7.3 264.9 %all-gather.3.cloned.1.call-start = ((), (), s32[]{:S(2)}) async-start(), calls=%async_computation.1 | async-start | bytes 13369344 | tf_op jit(solution)/shard_map/all_gather | solution.py:28
  12.3 11.5 %copy-start.1 = (s32[768]{0:T(1024)S(1)}, s32[768]{0:T(1024)}, u32[]{:S(2)}) copy-start(s32[768]{0:T(1024)} %param.9) | copy-start | bytes 9220
  12.3 92.5 %all-to-all-start = ((bf16[32,12,16,512]{3,2,1,0:T(8,128)(2,1)}), bf16[32,12,16,512]{3,2,1,0:T(8,128)(2,1)}, u32[]{:S(2)}, u32[]{:S(2)}) async-start(bf16[32,12,16,512]{3,2,1,0:T(8,128)(2,1)} %stack.2), calls=%async_computation | async-start | bytes 12582912 | tf_op jit(solution)/shard_map/all_to_all | solution.py:12
  127.4 7.1 %copy-start = (bf16[768,512]{1,0:T(8,128)(2,1)S(1)}, bf16[768,512]{1,0:T(8,128)(2,1)}, u32[]{:S(2)}) copy-start(bf16[768,512]{1,0:T(8,128)(2,1)} %param.5) | copy-start | bytes 2359300
Sparse Core Ops, SparseCore 0:
  10.5 103.2 all-gather.4
  115.9 156.2 all-gather.2
